TPU v7x, 32 devices: a whole 2x2x4 slice. The times are simulated.
32 devices in a mesh: group: 1, cent: 32 (over z, y, x, core).
Axes of the slice: x: 2, y: 2, z: 4, core: 2. Of those that a mesh axis runs over, the one named last changes fastest.
Arguments:
- embeddings: bfloat16 [12288, 768], P(('group', 'cent')), may hold values from -6 to 6
- assign: int32 [12288], P(('group', 'cent')), may hold values from 0 to 8191, as said below
- codes: int32 [12288, 96], P(('group', 'cent')), may hold values from 0 to 255
- centroids: bfloat16 [8192, 768], P(('group', 'cent')), may hold values from -6 to 6
- codebook: float32 [256, 768], P(('group', 'cent')), may hold values from -6 to 6
Outputs:
- residuals: bfloat16 [12288, 768], P(('group', 'cent'))
- new_centroids: float32 [8192, 768], P(('group', 'cent'))
- new_codebook: float32 [256, 768], P(('group', 'cent'))
Inputs may be any that keep to these rules, and one draw needn't show every extreme that they name: Among the rows of one device, at most 12 have assign // 256 equal to any one value, and in every draw each device has exactly 12 rows on one such value.
All inputs are finite; a program needn't handle non-finite values.
Results may differ from a plain program's by a relative error of at most 0.001.
Values may be sent and summed in bfloat16 or wider, within the bound.
A program may use at most 128 MiB of HBM per device.

v0:
```python
import jax
import jax.numpy as jnp
from jax import lax
from jax.sharding import PartitionSpec as P

CAP = 12


prior_weight = 16.0


def shards(embeddings, assign, codes, centroids, codebook):
    num_rows, width = embeddings.shape
    held = centroids.shape[0]
    peers = lax.axis_size("cent")
    slots = peers * CAP
    owner = assign // held
    local = assign - owner * held
    hits = (owner[:, None] == jnp.arange(peers, dtype=jnp.int32)[None, :]).astype(jnp.int32)
    rank = jnp.sum((jnp.cumsum(hits, axis=0) - 1) * hits, axis=1)
    slot_of = owner * CAP + rank
    place = (slot_of[None, :] == jnp.arange(slots, dtype=jnp.int32)[:, None]).astype(jnp.bfloat16)
    outgoing = jnp.dot(place, embeddings, preferred_element_type=jnp.float32).astype(jnp.bfloat16)
    labels = (local + 1).astype(jnp.bfloat16)
    slot_ids = jnp.dot(place, labels[:, None], preferred_element_type=jnp.float32).astype(
        jnp.bfloat16
    )
    received, recv_ids = (
        lax.all_to_all(
            outgoing.reshape(peers, CAP, width), "cent", split_axis=0, concat_axis=0, tiled=True
        ),
        lax.all_to_all(
            slot_ids.reshape(peers, CAP), "cent", split_axis=0, concat_axis=0, tiled=True
        ),
    )
    recv_rows = received.reshape(slots, width)
    recv_local = recv_ids.reshape(slots).astype(jnp.float32) - 1.0
    select = (recv_local[None, :] == jnp.arange(held, dtype=jnp.float32)[:, None]).astype(
        jnp.bfloat16
    )
    coarse_sums = jnp.dot(select, recv_rows, preferred_element_type=jnp.float32)
    coarse_counts = jnp.sum(select, axis=1, dtype=jnp.float32)
    new_centroids = (coarse_sums + prior_weight * centroids.astype(jnp.float32)) / (
        coarse_counts[:, None] + prior_weight
    )
    piece = lax.all_gather(centroids, "cent", axis=0, tiled=True)
    pick = (assign[:, None] == jnp.arange(piece.shape[0], dtype=jnp.int32)[None, :]).astype(
        jnp.bfloat16
    )
    chosen = jnp.dot(pick, piece, preferred_element_type=jnp.float32)
    residuals = (embeddings.astype(jnp.float32) - chosen).astype(jnp.bfloat16)
    subspaces = codes.shape[1]
    sub_width = width // subspaces
    words = codebook.shape[0] * peers
    shaped = residuals.reshape(num_rows, subspaces, sub_width)
    blocks = 8
    step_size = subspaces // blocks
    word_ids = jnp.arange(words, dtype=jnp.int32)
    sum_parts = []
    count_parts = []
    for block in range(blocks):
        lower = block * step_size
        block_codes = codes[:, lower : lower + step_size]
        onehot = (block_codes[:, :, None] == word_ids[None, None, :]).astype(jnp.bfloat16)
        part_sums = jnp.einsum(
            "rmc,rmj->cmj",
            onehot,
            shaped[:, lower : lower + step_size, :],
            preferred_element_type=jnp.float32,
        )
        sum_parts.append(part_sums)
        count_parts.append(jnp.sum(onehot, axis=0, dtype=jnp.float32).T)
    code_sums = jnp.concatenate(sum_parts, axis=1).reshape(words, width)
    code_counts = jnp.concatenate(count_parts, axis=1)
    mine = codebook.shape[0]
    total_sums, total_counts = lax.psum((code_sums, code_counts), "cent")
    begin = lax.axis_index("cent") * mine
    own_sums = lax.dynamic_slice_in_dim(total_sums, begin, mine, 0)
    own_counts = lax.dynamic_slice_in_dim(total_counts, begin, mine, 0)
    spread_counts = jnp.repeat(own_counts, sub_width, axis=1)
    new_codebook = (own_sums + prior_weight * codebook) / (spread_counts + prior_weight)
    return (residuals, new_centroids, new_codebook)


def solution(mesh):
    in_specs = (
        P(("group", "cent"), None),
        P(("group", "cent")),
        P(("group", "cent"), None),
        P(("group", "cent"), None),
        P(("group", "cent"), None),
    )
    out_specs = (P(("group", "cent"), None), P(("group", "cent"), None), P(("group", "cent"), None))
    return jax.shard_map(shards, mesh=mesh, in_specs=in_specs, out_specs=out_specs, check_vma=False)
```

profile of v0, /device:TPU:20, one launch (start us, length us, event | category | flops | bytes accessed | tf_op | source)
XLA Modules:
  0.0 272.5 jit_solution(15738675384005111487)
XLA Ops:
  8.6 0.9 reduce-window.6
  10.9 5.9 %all-to-all-start = ((bf16[32,1,12]{2,1,0:T(2,128)(2,1)}), bf16[32,1,12]{2,1,0:T(2,128)(2,1)S(1)}, u32[]{:S(2)}, u32[]{:S(2)}) async-start(bf16[32,1,12]{2,1,0:T(2,128)(2,1)} %all_to_all.12), calls=%async_computation | async-start | bytes 32768 | tf_op jit(solution)/shard_map/all_to_all | solution.py:32
  16.8 0.9 fusion.62
  17.7 1.8 convert_reduce_fusion.6
  19.7 1.7 convert_reduce_fusion.4
  21.4 1.8 convert_reduce_fusion.2
  23.2 1.8 convert_reduce_fusion
  24.9 1.5 convolution_convert_fusion
  27.2 1.0 reshape.74
  28.2 1.0 concatenate.7
  29.1 5.8 %all-to-all-start.1 = ((bf16[32,12,768]{2,1,0:T(8,128)(2,1)}), bf16[32,12,768]{2,1,0:T(8,128)(2,1)S(1)}, u32[]{:S(2)}, u32[]{:S(2)}) async-start(bf16[32,12,768]{2,1,0:T(8,128)(2,1)} %reshape.74), calls=%async_computation.1 | async-start | bytes 1572864 | tf_op jit(solution)/shard_map/all_to_all | solution.py:29
  35.5 82.5 %all-gather.2.cloned.1.call-done = bf16[8192,768]{1,0:T(8,128)(2,1)} async-done(((bf16[256,768]{1,0:T(8,128)(2,1)}), bf16[8192,768]{1,0:T(8,128)(2,1)}) %all-gather.2.cloned.1.call-update) | async-done | bytes 12582928 | tf_op jit(solution)/shard_map/all_gather | solution.py:46
  118.0 8.6 %fusion.27 = bf16[384,768]{1,0:T(8,128)(2,1)S(1)} fusion(bf16[8192,768]{1,0:T(8,128)(2,1)} %all-gather.2.cloned.1.call-done, s32[384]{0:T(512)S(1)} %copy-done.4, bf16[384,768]{1,0:T(8,128)(2,1)S(1)} %copy-done), kind=kOutput, calls=%fused_computation.44 | convolution fusion | flops 4835868672 | bytes 13764096 | tf_op jit(solution)/shard_map/dot_general | solution.py:50
  126.9 0.9 fusion.30
  127.8 0.9 fusion.32
  128.6 0.9 fusion.34
  129.5 0.9 fusion.36
  130.4 0.9 fusion.38
  131.3 0.9 fusion.40
  132.1 0.9 fusion.42
  133.9 1.2 copy.33
  135.3 1.2 fusion.28
  136.5 126.7 %all-reduce.3.cloned.1.call-done = (f32[256,96]{1,0:T(8,128)}, f32[256,768]{1,0:T(8,128)}) async-done(((f32[256,96]{1,0:T(8,128)}, f32[256,768]{1,0:T(8,128)}), (f32[256,96]{1,0:T(8,128)}, f32[256,768]{1,0:T(8,128)})) %all-reduce.3.cloned.1.call-update) | async-done | bytes 884752 | tf_op jit(solution)/shard_map/psum | solution.py:76
  264.3 1.4 add_divide_fusion
  (43 shorter events, 6.6 us)
Async XLA Ops:
  7.2 110.8 %copy-start.4 = (s32[384]{0:T(512)S(1)}, s32[384]{0:T(512)}, u32[]{:S(2)}) copy-start(s32[384]{0:T(512)} %param.6) | copy-start | bytes 4612
  7.2 110.8 %copy-start = (bf16[384,768]{1,0:T(8,128)(2,1)S(1)}, bf16[384,768]{1,0:T(8,128)(2,1)}, u32[]{:S(2)}) copy-start(bf16[384,768]{1,0:T(8,128)(2,1)} %param.5) | copy-start | bytes 1769476
  7.2 110.8 %all-gather.2.cloned.1.call-start = ((), (), s32[]{:S(2)}) async-start(), calls=%async_computation.2 | async-start | bytes 12976128 | tf_op jit(solution)/shard_map/all_gather | solution.py:46
  10.9 18.3 %all-to-all-start = ((bf16[32,1,12]{2,1,0:T(2,128)(2,1)}), bf16[32,1,12]{2,1,0:T(2,128)(2,1)S(1)}, u32[]{:S(2)}, u32[]{:S(2)}) async-start(bf16[32,1,12]{2,1,0:T(2,128)(2,1)} %all_to_all.12), calls=%async_computation | async-start | bytes 32768 | tf_op jit(solution)/shard_map/all_to_all | solution.py:32
  29.1 106.0 %all-to-all-start.1 = ((bf16[32,12,768]{2,1,0:T(8,128)(2,1)}), bf16[32,12,768]{2,1,0:T(8,128)(2,1)S(1)}, u32[]{:S(2)}, u32[]{:S(2)}) async-start(bf16[32,12,768]{2,1,0:T(8,128)(2,1)} %reshape.74), calls=%async_computation.1 | async-start | bytes 1572864 | tf_op jit(solution)/shard_map/all_to_all | solution.py:29
  35.0 228.3 %all-reduce.3.cloned.1.call-start = ((), (), s32[]{:S(2)}) async-start(), calls=%async_computation.3 | async-start | bytes 1835008 | tf_op jit(solution)/shard_map/psum | solution.py:76
  126.5 3.8 %copy-start.1 = (bf16[384,768]{1,0:T(8,128)(2,1)}, bf16[384,768]{1,0:T(8,128)(2,1)S(1)}, u32[]{:S(2)}) copy-start(bf16[384,768]{1,0:T(8,128)(2,1)S(1)} %fusion.27) | copy-start | bytes 1769476
  131.3 4.0 %copy-start.2 = (bf16[256,768]{1,0:T(8,128)(2,1)S(1)}, bf16[256,768]{1,0:T(8,128)(2,1)}, u32[]{:S(2)}) copy-start(bf16[256,768]{1,0:T(8,128)(2,1)} %param.8) | copy-start | bytes 1179652
  133.9 130.4 %copy-start.3 = (f32[8,768]{1,0:T(8,128)S(1)}, f32[8,768]{1,0:T(8,128)}, u32[]{:S(2)}) copy-start(f32[8,768]{1,0:T(8,128)} %param.9) | copy-start | bytes 73732
Sparse Core Ops, SparseCore 0:
  10.9 107.0 all-gather.1
  135.2 127.9 all-reduce.2
where the time goes:
time: 276 us; the launch traced here: 273 us
  waiting for transfers between devices  210 us (76%)
  matrix products  18.6 us (7%)
  between operations  14.2 us (5%)
  starting transfers between devices  12 us (4%)
  other arithmetic  11 us (4%)
  local copies, waits for them, and re-layouts  6.85 us (2%)
    psum x1, waiting for transfers between devices, shards(): total_sums, total_counts = lax.psum((code_sums, code_counts), 'cent')  127 us
    all_gather x1, waiting for transfers between devices, shards(): piece = lax.all_gather(centroids, 'cent', axis=0, tiled=True)  82.5 us
    dot_general x1, matrix products, shards(): chosen = jnp.dot(pick, piece, preferred_element_type=jnp.float32)  8.55 us
    dot_general x8, matrix products, shards(): jnp.einsum('rmc,rmj->cmj', onehot, shaped[:, lower:lower + step_size, :],...  7.02 us
    reduce_sum x4, other arithmetic, shards(): count_parts.append(jnp.sum(onehot, axis=0, dtype=jnp.float32).T)  7 us
    all_to_all x1, starting transfers between devices, shards(): lax.all_to_all(slot_ids.reshape(peers, CAP), 'cent', split_axis=0, concat...  5.89 us
    all_to_all x1, starting transfers between devices, shards(): lax.all_to_all(outgoing.reshape(peers, CAP, width), 'cent', split_axis=0,...  5.82 us
  transfers between devices with their start and end apart: 4, of which 2 were waited for; matrix products, arithmetic and copies ran while one was open for 12% of the time, Pallas kernels for 0%

commit v1 on v0

--- a/solution.py
+++ b/solution.py
@@ -43,11 +43,15 @@
     new_centroids = (coarse_sums + prior_weight * centroids.astype(jnp.float32)) / (
         coarse_counts[:, None] + prior_weight
     )
-    piece = lax.all_gather(centroids, "cent", axis=0, tiled=True)
-    pick = (assign[:, None] == jnp.arange(piece.shape[0], dtype=jnp.int32)[None, :]).astype(
+    pick = (recv_local[:, None] == jnp.arange(held, dtype=jnp.float32)[None, :]).astype(
         jnp.bfloat16
     )
-    chosen = jnp.dot(pick, piece, preferred_element_type=jnp.float32)
+    answers = jnp.dot(pick, centroids, preferred_element_type=jnp.float32).astype(jnp.bfloat16)
+    returned = lax.all_to_all(
+        answers.reshape(peers, CAP, width), "cent", split_axis=0, concat_axis=0, tiled=True
+    ).reshape(slots, width)
+    unplace = (slot_of[:, None] == jnp.arange(slots, dtype=jnp.int32)[None, :]).astype(jnp.bfloat16)
+    chosen = jnp.dot(unplace, returned, preferred_element_type=jnp.float32)
     residuals = (embeddings.astype(jnp.float32) - chosen).astype(jnp.bfloat16)
     subspaces = codes.shape[1]
     sub_width = width // subspaces
@@ -73,10 +77,11 @@
     code_sums = jnp.concatenate(sum_parts, axis=1).reshape(words, width)
     code_counts = jnp.concatenate(count_parts, axis=1)
     mine = codebook.shape[0]
-    total_sums, total_counts = lax.psum((code_sums, code_counts), "cent")
-    begin = lax.axis_index("cent") * mine
-    own_sums = lax.dynamic_slice_in_dim(total_sums, begin, mine, 0)
-    own_counts = lax.dynamic_slice_in_dim(total_counts, begin, mine, 0)
+    packed = jnp.concatenate([code_sums, code_counts], axis=1).reshape(peers, mine, -1)
+    blocks_in = lax.all_to_all(packed, "cent", split_axis=0, concat_axis=0, tiled=True)
+    totals = jnp.sum(blocks_in, axis=0)
+    own_sums = totals[:, :width]
+    own_counts = totals[:, width:]
     spread_counts = jnp.repeat(own_counts, sub_width, axis=1)
     new_codebook = (own_sums + prior_weight * codebook) / (spread_counts + prior_weight)
     return (residuals, new_centroids, new_codebook)

time: 276 us -> 106 us (0.38)
  the two profiles are of different devices: /device:TPU:20 before, /device:TPU:0 now
where the time goes in v1:
time: 106 us; the launch traced here: 105 us
  waiting for transfers between devices  34 us (32%)
  local copies, waits for them, and re-layouts  30.2 us (28%)
  starting transfers between devices  19.3 us (18%)
  matrix products  10.8 us (10%)
  other arithmetic  9.65 us (9%)
    concatenate x11, local copies, waits for them, and re-layouts, shards(): jnp.concatenate([code_sums, code_counts], axis=1).reshape(peers, mine, -1)  25.1 us
    all_to_all x1, waiting for transfers between devices, shards(): lax.all_to_all(packed, 'cent', split_axis=0, concat_axis=0, tiled=True)  21.9 us
    all_to_all x1, starting transfers between devices, shards(): lax.all_to_all(slot_ids.reshape(peers, CAP), 'cent', split_axis=0, concat...  7.3 us
    dot_general x8, matrix products, shards(): jnp.einsum('rmc,rmj->cmj', onehot, shaped[:, lower:lower + step_size, :],...  7.02 us
    reduce_sum x4, other arithmetic, shards(): count_parts.append(jnp.sum(onehot, axis=0, dtype=jnp.float32).T)  6.96 us
    all_to_all x1, waiting for transfers between devices, shards(): lax.all_to_all(slot_ids.reshape(peers, CAP), 'cent', split_axis=0, concat...  6.12 us
    all_to_all x1, waiting for transfers between devices, shards(): lax.all_to_all(answers.reshape(peers, CAP, width), 'cent', split_axis=0,...  5.96 us
    all_to_all x1, starting transfers between devices, shards(): lax.all_to_all(packed, 'cent', split_axis=0, concat_axis=0, tiled=True)  5.67 us
  transfers between devices with their start and end apart: 4, of which 3 were waited for; matrix products, arithmetic and copies ran while one was open for 42% of the time, Pallas kernels for 0%

profile of v1, /device:TPU:0, one launch (start us, length us, event | category | flops | bytes accessed | tf_op | source)
XLA Modules:
  0.0 104.9 jit_solution(3136537642452586728)
XLA Ops:
  1.4 0.9 reduce-window.6
  3.7 7.3 %all-to-all-start = ((bf16[32,1,12]{2,1,0:T(2,128)(2,1)}), bf16[32,1,12]{2,1,0:T(2,128)(2,1)S(1)}, u32[]{:S(2)}, u32[]{:S(2)}) async-start(bf16[32,1,12]{2,1,0:T(2,128)(2,1)} %all_to_all.20), calls=%async_computation | async-start | bytes 32768 | tf_op jit(solution)/shard_map/all_to_all | solution.py:32
  11.0 0.9 fusion.62
  11.9 6.1 %all-to-all-done = bf16[32,1,12]{2,1,0:T(2,128)(2,1)S(1)} async-done(((bf16[32,1,12]{2,1,0:T(2,128)(2,1)}), bf16[32,1,12]{2,1,0:T(2,128)(2,1)S(1)}, u32[]{:S(2)}, u32[]{:S(2)}) %all-to-all-start) | async-done | bytes 800 | tf_op jit(solution)/shard_map/all_to_all | solution.py:32
  18.2 1.4 %convolution_convert_fusion.1 = bf16[384,768]{1,0:T(8,128)(2,1)S(1)} fusion(bf16[256,768]{1,0:T(8,128)(2,1)} %param.8, f32[384]{0:T(512)S(1)} %sub.32), kind=kOutput, calls=%fused_computation.43 | convolution fusion | flops 151388160 | bytes 984576 | tf_op jit(solution)/shard_map/dot_general | solution.py:49
  19.6 1.0 reshape.96
  20.6 2.6 %all-to-all-start.1 = ((bf16[32,12,768]{2,1,0:T(8,128)(2,1)}), bf16[32,12,768]{2,1,0:T(8,128)(2,1)S(1)}, u32[]{:S(2)}, u32[]{:S(2)}) async-start(bf16[32,12,768]{2,1,0:T(8,128)(2,1)} %reshape.96), calls=%async_computation.1 | async-start | bytes 1572864 | tf_op jit(solution)/shard_map/all_to_all | solution.py:50
  23.2 1.8 %convert_reduce_fusion.6 = (f32[12,256]{1,0:T(8,128)S(1)}, f32[12,256]{1,0:T(8,128)S(1)}) fusion(s32[384,12]{0,1:T(8,128)S(1)} %get-tuple-element.10, s32[384,12]{0,1:T(8,128)S(1)} %get-tuple-element.11), kind=kLoop, calls=%fused_computation.6 | loop fusion | flops 9431040 | bytes 61440 | tf_op jit(solution)/shard_map/reduce_sum | solution.py:76
  26.5 1.7 %convert_reduce_fusion.4 = (f32[12,256]{1,0:T(8,128)S(1)}, f32[12,256]{1,0:T(8,128)S(1)}) fusion(s32[384,12]{0,1:T(8,128)S(1)} %get-tuple-element.8, s32[384,12]{0,1:T(8,128)S(1)} %get-tuple-element.9), kind=kLoop, calls=%fused_computation.4 | loop fusion | flops 9431040 | bytes 61440 | tf_op jit(solution)/shard_map/reduce_sum | solution.py:76
  29.8 1.7 %convert_reduce_fusion.2 = (f32[12,256]{1,0:T(8,128)S(1)}, f32[12,256]{1,0:T(8,128)S(1)}) fusion(s32[384,12]{0,1:T(8,128)S(1)} %get-tuple-element.6, s32[384,12]{0,1:T(8,128)S(1)} %get-tuple-element.7), kind=kLoop, calls=%fused_computation.2 | loop fusion | flops 9431040 | bytes 61440 | tf_op jit(solution)/shard_map/reduce_sum | solution.py:76
  33.0 1.7 %convert_reduce_fusion = (f32[12,256]{1,0:T(8,128)S(1)}, f32[12,256]{1,0:T(8,128)S(1)}) fusion(s32[384,12]{0,1:T(8,128)S(1)} %get-tuple-element.5, s32[384,12]{0,1:T(8,128)S(1)} %get-tuple-element.12), kind=kLoop, calls=%fused_computation | loop fusion | flops 9431040 | bytes 61440 | tf_op jit(solution)/shard_map/reduce_sum | solution.py:76
  36.8 1.1 %reshape.98 = bf16[32,12,768]{2,1,0:T(8,128)(2,1)} reshape(bf16[384,768]{1,0:T(8,128)(2,1)S(1)} %convolution_convert_fusion) | data formatting | bytes 1179648 | tf_op jit(solution)/shard_map/reshape | solution.py:30
  37.8 6.0 %all-to-all-done.1 = bf16[32,12,768]{2,1,0:T(8,128)(2,1)S(1)} async-done(((bf16[32,12,768]{2,1,0:T(8,128)(2,1)}), bf16[32,12,768]{2,1,0:T(8,128)(2,1)S(1)}, u32[]{:S(2)}, u32[]{:S(2)}) %all-to-all-start.1) | async-done | bytes 589856 | tf_op jit(solution)/shard_map/all_to_all | solution.py:50
  43.8 3.7 %all-to-all-start.2 = ((bf16[32,12,768]{2,1,0:T(8,128)(2,1)}), bf16[32,12,768]{2,1,0:T(8,128)(2,1)S(1)}, u32[]{:S(2)}, u32[]{:S(2)}) async-start(bf16[32,12,768]{2,1,0:T(8,128)(2,1)} %reshape.98), calls=%async_computation.2 | async-start | bytes 1572864 | tf_op jit(solution)/shard_map/all_to_all | solution.py:29
  48.6 0.9 fusion.27
  49.5 0.9 fusion.29
  51.2 0.9 fusion.33
  52.1 0.9 fusion.35
  55.6 8.6 %reshape.103 = f32[32,8,768]{1,0,2:T(8,128)} reshape(f32[256,96,8]{0,2,1:T(8,128)S(1)} %fusion.41) | data formatting | bytes 1572864 | tf_op jit(solution)/shard_map/concatenate | solution.py:80
  64.2 9.1 %copy.51 = f32[32,8,768]{2,1,0:T(8,128)S(1)} copy(f32[32,8,768]{1,0,2:T(8,128)} %reshape.103) | data formatting | bytes 1572864 | tf_op jit(solution)/shard_map/concatenate | solution.py:80
  73.4 1.3 %concatenate.35 = f32[32,8,864]{2,1,0:T(8,128)} concatenate(f32[32,8,768]{2,1,0:T(8,128)S(1)} %copy.51, f32[32,8,12]{2,1,0:T(8,128)S(1)} %bitcast.89, f32[32,8,12]{2,1,0:T(8,128)S(1)} %bitcast.90, f32[32,8,12]{2,1,0:T(8,128)S(1)} %bitcast.91, f32[32,8,12]{2,1,0:T(8,128)S(1)} %bitcast.92, f32[32,8,12]{2,1,0:T(8,128)S(1)} %bitcast.93, f32[32,8,12]{2,1,0:T(8,128)S(1)} %bitcast.94, ...), dimensions={2} | concatenate | bytes 1769472 | tf_op jit(solution)/shard_map/concatenate | solution.py:80
  74.7 5.7 %all-to-all-start.3 = ((f32[32,8,864]{2,1,0:T(8,128)}), f32[32,8,864]{2,1,0:T(8,128)S(1)}, u32[]{:S(2)}, u32[]{:S(2)}) async-start(f32[32,8,864]{2,1,0:T(8,128)} %concatenate.35), calls=%async_computation.3 | async-start | bytes 1835008 | tf_op jit(solution)/shard_map/all_to_all | solution.py:81
  80.7 1.2 %fusion.25 = f32[256,768]{1,0:T(8,128)} fusion(bf16[384,768]{1,0:T(8,128)(2,1)S(1)} %reshape.99, bf16[256,768]{1,0:T(8,128)(2,1)S(1)} %copy-done.10, f32[256]{0:T(256)S(1)} %broadcast_add_fusion, f32[384]{0:T(512)S(1)} %sub.32), kind=kOutput, calls=%fused_computation.45 | convolution fusion | flops 151879680 | bytes 1772032 | tf_op jit(solution)/shard_map/dot_general | solution.py:41
  82.0 21.9 %all-to-all-done.3 = f32[32,8,864]{2,1,0:T(8,128)S(1)} async-done(((f32[32,8,864]{2,1,0:T(8,128)}), f32[32,8,864]{2,1,0:T(8,128)S(1)}, u32[]{:S(2)}, u32[]{:S(2)}) %all-to-all-start.3) | async-done | bytes 884768 | tf_op jit(solution)/shard_map/all_to_all | solution.py:81
  (80 shorter events, 14.7 us)
Async XLA Ops:
  0.6 35.7 %copy-start = (bf16[384,768]{1,0:T(8,128)(2,1)S(1)}, bf16[384,768]{1,0:T(8,128)(2,1)}, u32[]{:S(2)}) copy-start(bf16[384,768]{1,0:T(8,128)(2,1)} %param.5) | copy-start | bytes 1769476
  3.7 14.4 %all-to-all-start = ((bf16[32,1,12]{2,1,0:T(2,128)(2,1)}), bf16[32,1,12]{2,1,0:T(2,128)(2,1)S(1)}, u32[]{:S(2)}, u32[]{:S(2)}) async-start(bf16[32,1,12]{2,1,0:T(2,128)(2,1)} %all_to_all.20), calls=%async_computation | async-start | bytes 32768 | tf_op jit(solution)/shard_map/all_to_all | solution.py:32
  11.9 23.7 %copy-start.11 = (s32[384,12]{0,1:T(8,128)}, s32[384,12]{0,1:T(8,128)S(1)}, u32[]{:S(2)}) copy-start(s32[384,12]{0,1:T(8,128)S(1)} %get-tuple-element.7) | copy-start | bytes 55300
  11.9 23.7 %copy-start.13 = (s32[384,12]{0,1:T(8,128)}, s32[384,12]{0,1:T(8,128)S(1)}, u32[]{:S(2)}) copy-start(s32[384,12]{0,1:T(8,128)S(1)} %get-tuple-element.8) | copy-start | bytes 55300
  11.9 23.7 %copy-start.15 = (s32[384,12]{0,1:T(8,128)}, s32[384,12]{0,1:T(8,128)S(1)}, u32[]{:S(2)}) copy-start(s32[384,12]{0,1:T(8,128)S(1)} %get-tuple-element.9) | copy-start | bytes 55300
  11.9 23.7 %copy-start.17 = (s32[384,12]{0,1:T(8,128)}, s32[384,12]{0,1:T(8,128)S(1)}, u32[]{:S(2)}) copy-start(s32[384,12]{0,1:T(8,128)S(1)} %get-tuple-element.10) | copy-start | bytes 55300
  11.9 23.6 %copy-start.19 = (s32[384,12]{0,1:T(8,128)}, s32[384,12]{0,1:T(8,128)S(1)}, u32[]{:S(2)}) copy-start(s32[384,12]{0,1:T(8,128)S(1)} %get-tuple-element.11) | copy-start | bytes 55300
  20.6 23.2 %all-to-all-start.1 = ((bf16[32,12,768]{2,1,0:T(8,128)(2,1)}), bf16[32,12,768]{2,1,0:T(8,128)(2,1)S(1)}, u32[]{:S(2)}, u32[]{:S(2)}) async-start(bf16[32,12,768]{2,1,0:T(8,128)(2,1)} %reshape.96), calls=%async_computation.1 | async-start | bytes 1572864 | tf_op jit(solution)/shard_map/all_to_all | solution.py:50
  37.8 10.7 %copy-start.20 = (s32[384,12]{0,1:T(8,128)S(1)}, s32[384,12]{0,1:T(8,128)}, u32[]{:S(2)}) copy-start(s32[384,12]{0,1:T(8,128)} %copy-done.19) | copy-start | bytes 55300
  37.8 11.6 %copy-start.18 = (s32[384,12]{0,1:T(8,128)S(1)}, s32[384,12]{0,1:T(8,128)}, u32[]{:S(2)}) copy-start(s32[384,12]{0,1:T(8,128)} %copy-done.17) | copy-start | bytes 55300
  43.8 30.9 %all-to-all-start.2 = ((bf16[32,12,768]{2,1,0:T(8,128)(2,1)}), bf16[32,12,768]{2,1,0:T(8,128)(2,1)S(1)}, u32[]{:S(2)}, u32[]{:S(2)}) async-start(bf16[32,12,768]{2,1,0:T(8,128)(2,1)} %reshape.98), calls=%async_computation.2 | async-start | bytes 1572864 | tf_op jit(solution)/shard_map/all_to_all | solution.py:29
  48.2 3.9 %copy-start.1 = (bf16[384,768]{1,0:T(8,128)(2,1)}, bf16[384,768]{1,0:T(8,128)(2,1)S(1)}, u32[]{:S(2)}) copy-start(bf16[384,768]{1,0:T(8,128)(2,1)S(1)} %fusion.24) | copy-start | bytes 1769476
  48.2 3.9 %copy-start.12 = (s32[384,12]{0,1:T(8,128)S(1)}, s32[384,12]{0,1:T(8,128)}, u32[]{:S(2)}) copy-start(s32[384,12]{0,1:T(8,128)} %copy-done.11) | copy-start | bytes 55300
  64.2 9.2 %copy-start.2 = (f32[256,12]{1,0:T(8,128)S(1)}, f32[256,12]{1,0:T(8,128)}, u32[]{:S(2)}) copy-start(f32[256,12]{1,0:T(8,128)} %copy.52) | copy-start | bytes 36868
  64.2 9.2 %copy-start.3 = (f32[256,12]{1,0:T(8,128)S(1)}, f32[256,12]{1,0:T(8,128)}, u32[]{:S(2)}) copy-start(f32[256,12]{1,0:T(8,128)} %copy.53) | copy-start | bytes 36868
  64.2 9.2 %copy-start.4 = (f32[256,12]{1,0:T(8,128)S(1)}, f32[256,12]{1,0:T(8,128)}, u32[]{:S(2)}) copy-start(f32[256,12]{1,0:T(8,128)} %copy.54) | copy-start | bytes 36868
  64.2 9.2 %copy-start.5 = (f32[256,12]{1,0:T(8,128)S(1)}, f32[256,12]{1,0:T(8,128)}, u32[]{:S(2)}) copy-start(f32[256,12]{1,0:T(8,128)} %copy.55) | copy-start | bytes 36868
  64.2 9.2 %copy-start.6 = (f32[256,12]{1,0:T(8,128)S(1)}, f32[256,12]{1,0:T(8,128)}, u32[]{:S(2)}) copy-start(f32[256,12]{1,0:T(8,128)} %copy.56) | copy-start | bytes 36868
  64.2 9.2 %copy-start.7 = (f32[256,12]{1,0:T(8,128)S(1)}, f32[256,12]{1,0:T(8,128)}, u32[]{:S(2)}) copy-start(f32[256,12]{1,0:T(8,128)} %copy.57) | copy-start | bytes 36868
  64.2 9.2 %copy-start.8 = (f32[256,12]{1,0:T(8,128)S(1)}, f32[256,12]{1,0:T(8,128)}, u32[]{:S(2)}) copy-start(f32[256,12]{1,0:T(8,128)} %copy.58) | copy-start | bytes 36868
  64.2 9.2 %copy-start.9 = (f32[256,12]{1,0:T(8,128)S(1)}, f32[256,12]{1,0:T(8,128)}, u32[]{:S(2)}) copy-start(f32[256,12]{1,0:T(8,128)} %copy.59) | copy-start | bytes 36868
  73.3 7.4 %copy-start.10 = (bf16[256,768]{1,0:T(8,128)(2,1)S(1)}, bf16[256,768]{1,0:T(8,128)(2,1)}, u32[]{:S(2)}) copy-start(bf16[256,768]{1,0:T(8,128)(2,1)} %param.8) | copy-start | bytes 1179652
  74.7 29.6 %copy-start.21 = (f32[8,768]{1,0:T(8,128)S(1)}, f32[8,768]{1,0:T(8,128)}, u32[]{:S(2)}) copy-start(f32[8,768]{1,0:T(8,128)} %param.9) | copy-start | bytes 73732
  74.7 29.1 %all-to-all-start.3 = ((f32[32,8,864]{2,1,0:T(8,128)}), f32[32,8,864]{2,1,0:T(8,128)S(1)}, u32[]{:S(2)}, u32[]{:S(2)}) async-start(f32[32,8,864]{2,1,0:T(8,128)} %concatenate.35), calls=%async_computation.3 | async-start | bytes 1835008 | tf_op jit(solution)/shard_map/all_to_all | solution.py:81
  (2 other events, 6.3 us)

commit v2 on v0

v2 whole, which is shorter than its diff:
```python
import functools

import jax
import jax.numpy as jnp
from jax import lax
from jax.experimental import pallas as pl
from jax.experimental.pallas import tpu as pltpu
from jax.sharding import PartitionSpec as P

CAP = 12
PAD = 16
LANES = 128

prior_weight = 16.0
f32 = jnp.float32
bf16 = jnp.bfloat16


def dot(a, b, ca=1, cb=0, **kw):
    return lax.dot_general(
        a, b, (((ca,), (cb,)), ((), ())), preferred_element_type=f32, **kw
    )


def step_kernel(
    peers,
    assign_ref,
    emb_ref,
    codes_ref,
    cent_ref,
    book_ref,
    resid_ref,
    newc_ref,
    newb_ref,
    ids_s,
    ids_r,
    ans_s,
    ans_r,
    rows_s,
    rows_r,
    sum_s,
    sum_r,
    place_s,
    codes_t,
    res_s,
    send_sem,
    recv_sem,
):
    me = lax.axis_index("cent")
    num_rows, width = emb_ref.shape
    subspaces = codes_ref.shape[1]
    sub_width = width // subspaces
    held = cent_ref.shape[0]
    mine = book_ref.shape[0]
    words = mine * peers
    slots = peers * PAD


    barrier = pltpu.get_barrier_semaphore()

    def greet(d, carry):
        peer = lax.rem(me + d, peers)
        pl.semaphore_signal(barrier, inc=1, device_id={"cent": peer})
        return carry

    lax.fori_loop(1, peers, greet, 0)

    def cut(ref, index, rows):
        return ref.at[index] if rows is None else ref.at[index, pl.ds(0, rows)]

    def exchange(src, dst, k, rows):
        pltpu.make_async_copy(cut(src, me, rows), cut(dst, me, rows), recv_sem.at[k]).start()

        def send(d, carry):
            peer = lax.rem(me + d, peers)
            pltpu.make_async_remote_copy(
                src_ref=cut(src, peer, rows),
                dst_ref=cut(dst, me, rows),
                send_sem=send_sem.at[k],
                recv_sem=recv_sem.at[k],
                device_id={"cent": peer},
            ).start()
            return carry

        lax.fori_loop(1, peers, send, 0)

    def whole(ref, count, rows):
        if rows is None:
            return ref.at[pl.ds(0, count)]
        return ref.at[pl.ds(0, count), pl.ds(0, rows)]

    def arrived(dst, k, rows):
        pltpu.make_async_copy(
            whole(dst, peers, rows), whole(dst, peers, rows), recv_sem.at[k]
        ).wait()

    def sent(src, k, rows):
        pltpu.make_async_copy(
            whole(src, peers - 1, rows), whole(src, peers - 1, rows), send_sem.at[k]
        ).wait()

    a = assign_ref[...]
    peer_ids = lax.broadcasted_iota(jnp.int32, (peers, num_rows), 0)
    low = peer_ids * held
    hits = ((a >= low) & (a < low + held)).astype(f32)
    before = (
        lax.broadcasted_iota(jnp.int32, (num_rows, num_rows), 0)
        < lax.broadcasted_iota(jnp.int32, (num_rows, num_rows), 1)
    ).astype(f32).astype(bf16)
    earlier = dot(hits.astype(bf16), before)
    rank = jnp.sum(earlier * hits, axis=0, keepdims=True)
    owner = jnp.sum(peer_ids.astype(f32) * hits, axis=0, keepdims=True)
    slot_of = (owner * PAD + rank).astype(jnp.int32)
    label = a.astype(f32) - owner * held + 1.0
    place = (lax.broadcasted_iota(jnp.int32, (slots, num_rows), 0) == slot_of).astype(f32).astype(bf16)
    place_s[...] = place
    ids = dot(place, jnp.broadcast_to(label, (LANES, num_rows)).astype(bf16), 1, 1)
    ids_s[...] = ids.astype(bf16).reshape(peers, PAD, LANES)

    pl.semaphore_wait(barrier, peers - 1)
    exchange(ids_s, ids_r, 0, None)

    shifted = (codes_ref[...] + 1).astype(f32).astype(bf16)
    codes_t[...] = dot(shifted, place, 0, 1)
    rows_s[...] = dot(place, emb_ref[...]).astype(bf16).reshape(peers, PAD, width)

    arrived(ids_r, 0, None)
    got = ids_r[...].reshape(slots, LANES).astype(f32)
    lane = lax.broadcasted_iota(jnp.int32, (slots, LANES), 1).astype(f32)
    pick = jnp.concatenate(
        [(got == lane + (1.0 + LANES * i)).astype(f32).astype(bf16) for i in range(held // LANES)],
        axis=1,
    )
    ans_s[...] = dot(pick, cent_ref[...]).astype(bf16).reshape(peers, PAD, width)
    exchange(ans_s, ans_r, 1, None)
    exchange(rows_s, rows_r, 2, None)

    arrived(ans_r, 1, None)
    res_s[...] = (
        rows_s[...].reshape(slots, width).astype(f32) - ans_r[...].reshape(slots, width).astype(f32)
    ).astype(bf16)

    per = LANES // sub_width
    word = lax.broadcasted_iota(jnp.int32, (words, slots), 0).astype(f32).astype(bf16) + 1.0
    word = word.astype(bf16)
    lanes = lax.broadcasted_iota(jnp.int32, (words, LANES), 1)
    ones = jnp.ones((slots, LANES), bf16)
    counts = jnp.zeros((words, LANES), f32)
    for t in range(width // LANES):
        rhs = jnp.concatenate([res_s[:, t * LANES : (t + 1) * LANES], ones], axis=1)

        def one(u, carry, rhs=rhs, t=t):
            acc, cnt = carry
            m = t * per + u
            code = jnp.broadcast_to(codes_t[pl.ds(m, 1), :], (words, slots)).astype(bf16)
            onehot = jnp.where(code == word, jnp.ones_like(word), jnp.zeros_like(word))
            prod = dot(onehot, rhs)
            first = u * sub_width
            acc = jnp.where((lanes >= first) & (lanes < first + sub_width), prod[:, :LANES], acc)
            cnt = jnp.where(lanes == m, prod[:, LANES:], cnt)
            return acc, cnt

        acc, counts = lax.fori_loop(
            0, per, one, (jnp.zeros((words, LANES), f32), counts), unroll=4
        )
        put(sum_s, t, acc, peers, mine)
    put(sum_s, width // LANES, counts, peers, mine)
    exchange(sum_s, sum_r, 3, None)

    resid_ref[...] = dot(place_s[...], res_s[...], 0, 0).astype(bf16)
    arrived(rows_r, 2, None)
    coarse = dot(pick, rows_r[...].reshape(slots, width), 0, 0)
    held_counts = dot(pick, ones, 0, 0) + prior_weight
    for t in range(width // LANES):
        at = slice(t * LANES, (t + 1) * LANES)
        newc_ref[:, at] = (coarse[:, at] + prior_weight * cent_ref[:, at].astype(f32)) / held_counts

    arrived(sum_r, 3, None)
    totals = jnp.sum(sum_r[...], axis=0)
    col = lax.broadcasted_iota(jnp.int32, (LANES, width), 1)
    row = lax.broadcasted_iota(jnp.int32, (LANES, width), 0) * sub_width
    expand = ((col >= row) & (col < row + sub_width)).astype(f32)
    spread = dot(totals[:, width:], expand, precision=lax.Precision.HIGHEST)
    newb_ref[...] = (totals[:, :width] + prior_weight * book_ref[...]) / (spread + prior_weight)
    sent(ids_s, 0, None)
    sent(ans_s, 1, None)
    sent(rows_s, 2, None)
    sent(sum_s, 3, None)


def put(ref, t, value, peers, mine):
    at = slice(t * LANES, (t + 1) * LANES)
    if mine % 8 == 0:
        ref[:, :, at] = value.reshape(peers, mine, LANES)
    else:
        for p in range(peers):
            ref[p, :, at] = value[p * mine : (p + 1) * mine]


def shards(embeddings, assign, codes, centroids, codebook):
    num_rows, width = embeddings.shape
    held = centroids.shape[0]
    mine = codebook.shape[0]
    subspaces = codes.shape[1]
    peers = lax.axis_size("cent")
    slots = peers * PAD
    vmem = pl.BlockSpec(memory_space=pltpu.VMEM)
    return pl.pallas_call(
        functools.partial(step_kernel, peers),
        out_shape=(
            jax.ShapeDtypeStruct((num_rows, width), bf16),
            jax.ShapeDtypeStruct((held, width), f32),
            jax.ShapeDtypeStruct((mine, width), f32),
        ),
        in_specs=[vmem] * 5,
        out_specs=(vmem,) * 3,
        scratch_shapes=[
            pltpu.VMEM((peers, PAD, LANES), bf16),
            pltpu.VMEM((peers, PAD, LANES), bf16),
            pltpu.VMEM((peers, PAD, width), bf16),
            pltpu.VMEM((peers, PAD, width), bf16),
            pltpu.VMEM((peers, PAD, width), bf16),
            pltpu.VMEM((peers, PAD, width), bf16),
            pltpu.VMEM((peers, mine, width + LANES), f32),
            pltpu.VMEM((peers, mine, width + LANES), f32),
            pltpu.VMEM((slots, num_rows), bf16),
            pltpu.VMEM((subspaces, slots), f32),
            pltpu.VMEM((slots, width), bf16),
            pltpu.SemaphoreType.DMA((4,)),
            pltpu.SemaphoreType.DMA((4,)),
        ],
        compiler_params=pltpu.CompilerParams(
            collective_id=0, has_side_effects=True, vmem_limit_bytes=48 * 1024 * 1024
        ),
    )(assign.reshape(1, num_rows), embeddings, codes, centroids, codebook)


def solution(mesh):
    spec = P(("group", "cent"), None)
    in_specs = (spec, P(("group", "cent")), spec, spec, spec)
    return jax.shard_map(
        shards, mesh=mesh, in_specs=in_specs, out_specs=(spec, spec, spec), check_vma=False
    )
```

time: 276 us -> 73 us (0.26)
  the two profiles are of different devices: /device:TPU:20 before, /device:TPU:13 now
where the time goes in v2:
time: 73 us; the launch traced here: 72.7 us
  Pallas kernels  66 us (90%)
  local copies, waits for them, and re-layouts  6.09 us (8%)
    pallas_call x1, Pallas kernels, shards(): pl.pallas_call(functools.partial(step_kernel, peers), out_shape=(jax.Shap...  66 us
    unnamed x10, local copies, waits for them, and re-layouts  5.4 us

profile of v2, /device:TPU:13, one launch (start us, length us, event | category | flops | bytes accessed | tf_op | source)
XLA Modules:
  0.0 72.7 jit_solution(5375511954019632700)
XLA Ops:
  0.6 0.7 reshape.9.assign_ref
  1.3 0.0 copy-start.2
  1.3 1.0 %copy.8.codes_ref = s32[384,96]{1,0:T(8,128)S(1)} copy(s32[384,96]{0,1:T(8,128)} %param.7) | data formatting | bytes 294912 | tf_op args[2]
  2.4 0.0 copy-done.2
  2.4 0.0 copy-start
  2.4 1.1 %copy-done = bf16[384,768]{1,0:T(8,128)(2,1)S(1)} copy-done((bf16[384,768]{1,0:T(8,128)(2,1)S(1)}, bf16[384,768]{1,0:T(8,128)(2,1)}, u32[]{:S(2)}) %copy-start) | copy-done | bytes 589848
  3.4 0.0 copy-start.1
  3.4 1.0 %copy-done.1 = bf16[256,768]{1,0:T(8,128)(2,1)S(1)} copy-done((bf16[256,768]{1,0:T(8,128)(2,1)S(1)}, bf16[256,768]{1,0:T(8,128)(2,1)}, u32[]{:S(2)}) %copy-start.1) | copy-done | bytes 393240
  4.4 66.0 %shard_map.76 = (bf16[384,768]{1,0:T(8,128)(2,1)S(1)}, f32[256,768]{1,0:T(8,128)S(1)}, f32[8,768]{1,0:T(8,128)S(1)}) custom-call(s32[1,384]{1,0:T(1,128)S(1)} %reshape.9.assign_ref, bf16[384,768]{1,0:T(8,128)(2,1)S(1)} %copy-done, s32[384,96]{1,0:T(8,128)S(1)} %copy.8.codes_ref, bf16[256,768]{1,0:T(8,128)(2,1)S(1)} %copy-done.1, f32[8,768]{1,0:T(8,128)S(1)} %copy-done.2), custom_call_target="tpu_custom_call" | custom-call | tf_op jit(solution)/shard_map/pallas_call | solution.py:208
  70.4 0.8 %copy.12 = bf16[384,768]{1,0:T(8,128)(2,1)} copy(bf16[384,768]{1,0:T(8,128)(2,1)S(1)} %get-tuple-element.6) | data formatting | bytes 1179648
  71.2 0.9 %copy.13 = f32[256,768]{1,0:T(8,128)} copy(f32[256,768]{1,0:T(8,128)S(1)} %get-tuple-element.7) | data formatting | bytes 1572864
  72.1 0.6 copy.14
Async XLA Ops:
  1.3 1.0 %copy-start.2 = (f32[8,768]{1,0:T(8,128)S(1)}, f32[8,768]{1,0:T(8,128)}, u32[]{:S(2)}) copy-start(f32[8,768]{1,0:T(8,128)} %book_ref.1) | copy-start | bytes 73732
  2.4 1.1 %copy-start = (bf16[384,768]{1,0:T(8,128)(2,1)S(1)}, bf16[384,768]{1,0:T(8,128)(2,1)}, u32[]{:S(2)}) copy-start(bf16[384,768]{1,0:T(8,128)(2,1)} %emb_ref.1) | copy-start | bytes 1769476
  3.4 1.0 %copy-start.1 = (bf16[256,768]{1,0:T(8,128)(2,1)S(1)}, bf16[256,768]{1,0:T(8,128)(2,1)}, u32[]{:S(2)}) copy-start(bf16[256,768]{1,0:T(8,128)(2,1)} %cent_ref.1) | copy-start | bytes 1179652

commit v3 on v2

v3 whole, which is shorter than its diff:
```python
import functools

import jax
import jax.numpy as jnp
from jax import lax
from jax.experimental import pallas as pl
from jax.experimental.pallas import tpu as pltpu
from jax.sharding import PartitionSpec as P

CAP = 12
FULL = 8
REST = CAP - FULL
EARLY = 9
LANES = 128

prior_weight = 16.0
f32 = jnp.float32
bf16 = jnp.bfloat16


def dot(a, b, ca=1, cb=0, **kw):
    return lax.dot_general(
        a, b, (((ca,), (cb,)), ((), ())), preferred_element_type=f32, **kw
    )


def step_kernel(
    peers,
    assign_ref,
    emb_ref,
    codes_ref,
    cent_ref,
    book_ref,
    resid_ref,
    newc_ref,
    newb_ref,
    ids_s,
    ids_r,
    ans_s,
    ans_r,
    rows_s,
    rows_r,
    pair_s,
    pair_r,
    sum_s,
    sum_r,
    place_s,
    codes_t,
    res_s,
    send_sem,
    recv_sem,
    pair_send,
    pair_recv,
):
    me = lax.axis_index("cent")
    num_rows, width = emb_ref.shape
    half = width // 2
    subspaces = codes_ref.shape[1]
    sub_width = width // subspaces
    held = cent_ref.shape[0]
    mine = book_ref.shape[0]
    words = mine * peers
    slots = peers * FULL
    chips = peers // 2
    core = lax.rem(me, 2)
    chip = lax.div(me, 2)
    tiles = width // LANES

    barrier = pltpu.get_barrier_semaphore()

    def greet(d, carry):
        peer = lax.rem(me + d, peers)
        pl.semaphore_signal(barrier, inc=1, device_id={"cent": peer})
        return carry

    lax.fori_loop(1, peers, greet, 0)

    def start_own(src, dst, k, index):
        pltpu.make_async_copy(src.at[index], dst.at[index], recv_sem.at[k]).start()

    def start_sends(src, dst, k, first, last):
        def send(d, carry):
            peer = lax.rem(me + d, peers)
            pltpu.make_async_remote_copy(
                src_ref=src.at[peer],
                dst_ref=dst.at[me],
                send_sem=send_sem.at[k],
                recv_sem=recv_sem.at[k],
                device_id={"cent": peer},
            ).start()
            return carry

        lax.fori_loop(first, last, send, 0)

    def arrived(dst, k):
        pltpu.make_async_copy(dst, dst, recv_sem.at[k]).wait()

    def sent(src, k):
        part = src.at[pl.ds(0, src.shape[0] - 1)]
        pltpu.make_async_copy(part, part, send_sem.at[k]).wait()

    a = assign_ref[...]
    peer_ids = lax.broadcasted_iota(jnp.int32, (peers, num_rows), 0)
    low = peer_ids * held
    hits = ((a >= low) & (a < low + held)).astype(f32)
    before = (
        lax.broadcasted_iota(jnp.int32, (num_rows, num_rows), 0)
        < lax.broadcasted_iota(jnp.int32, (num_rows, num_rows), 1)
    ).astype(f32).astype(bf16)
    earlier = dot(hits.astype(bf16), before)
    rank = jnp.sum(earlier * hits, axis=0, keepdims=True).astype(jnp.int32)
    owner = jnp.sum(peer_ids.astype(f32) * hits, axis=0, keepdims=True).astype(jnp.int32)
    label = (a - owner * held + 1).astype(f32)
    labels = jnp.broadcast_to(label, (LANES, num_rows)).astype(bf16)
    slot_ids = lax.broadcasted_iota(jnp.int32, (slots, num_rows), 0)
    base = owner * FULL + rank
    late = rank >= FULL
    targets = (
        jnp.where(late, -1, base),
        jnp.where(late, base - FULL, -1),
        jnp.where(late, base - (FULL - REST), -1),
    )
    places = [(slot_ids == target).astype(f32).astype(bf16) for target in targets]
    for i in range(3):
        place_s[i] = places[i]
    ids_s[:, :, :LANES] = dot(places[0], labels, 1, 1).astype(bf16).reshape(peers, FULL, LANES)
    ids_s[:, :, LANES:] = (
        dot(places[1] + places[2], labels, 1, 1).astype(bf16).reshape(peers, FULL, LANES)
    )

    pl.semaphore_wait(barrier, peers - 1)
    start_own(ids_s, ids_r, 0, me)
    start_sends(ids_s, ids_r, 0, 1, peers)

    emb = emb_ref[...]
    rows_s[:, :, :width] = dot(places[0], emb).astype(bf16).reshape(peers, FULL, width)
    rows_s[:, :, width:] = (
        (dot(places[1], emb[:, :half]) + dot(places[2], emb[:, half:]))
        .astype(bf16)
        .reshape(peers, FULL, half)
    )
    start_own(rows_s, rows_r, 2, me)
    start_sends(rows_s, rows_r, 2, 1, EARLY)
    shifted = (codes_ref[...] + 1).astype(f32).astype(bf16)
    lower = lax.broadcasted_iota(jnp.int32, (subspaces, slots), 0) < subspaces // 2
    codes_t[:, :slots] = dot(shifted, places[0], 0, 1)
    codes_t[:, slots:] = jnp.where(
        lower, dot(shifted, places[1], 0, 1), dot(shifted, places[2], 0, 1)
    )

    arrived(ids_r, 0)
    lane = lax.broadcasted_iota(jnp.int32, (slots, LANES), 1).astype(f32)

    def pick_of(got):
        got = got.reshape(slots, LANES).astype(f32)
        return jnp.concatenate(
            [
                (got == lane + (1.0 + LANES * i)).astype(f32).astype(bf16)
                for i in range(held // LANES)
            ],
            axis=1,
        )

    pick_a = pick_of(ids_r[:, :, :LANES])
    got_b = ids_r[:, :, LANES:]
    front = lax.broadcasted_iota(jnp.int32, got_b.shape, 1) < REST
    pick_b = pick_of(jnp.where(front, got_b.astype(f32), 0.0))
    pick_c = pick_of(jnp.where(front, 0.0, got_b.astype(f32)))
    cent = cent_ref[...]
    ans_s[:, :, :width] = dot(pick_a, cent).astype(bf16).reshape(peers, FULL, width)
    ans_s[:, :, width:] = (
        (dot(pick_b, cent[:, :half]) + dot(pick_c, cent[:, half:]))
        .astype(bf16)
        .reshape(peers, FULL, half)
    )
    start_own(ans_s, ans_r, 1, me)
    start_sends(ans_s, ans_r, 1, 1, peers)
    start_sends(rows_s, rows_r, 2, EARLY, peers)

    arrived(ans_r, 1)
    res_s[...] = (
        rows_s[...].reshape(slots, width + half).astype(f32)
        - ans_r[...].reshape(slots, width + half).astype(f32)
    ).astype(bf16)

    per = LANES // sub_width
    word = (lax.broadcasted_iota(jnp.int32, (words, 2 * slots), 0) + 1).astype(f32).astype(bf16)
    lanes = lax.broadcasted_iota(jnp.int32, (words, LANES), 1)
    ones = jnp.ones((2 * slots, LANES), bf16)
    counts = jnp.zeros((words, LANES), f32)

    def pair_copy(t):
        return pltpu.make_async_remote_copy(
            src_ref=pair_s.at[t, 1 - core],
            dst_ref=pair_r.at[t],
            send_sem=pair_send.at[t],
            recv_sem=pair_recv.at[t],
            device_id={"cent": me + 1 - 2 * core},
        )

    def put(t, value):
        if mine % 8 == 0:
            split = value.reshape(chips, 2, mine, LANES)
            for c in range(2):
                pair_s[t, c] = split[:, c]
        else:
            for p in range(peers):
                pair_s[t, p % 2, p // 2] = value[p * mine : (p + 1) * mine]
        pair_copy(t).start()

    for t in range(tiles):
        at = t * LANES
        beside = width + at % half
        rhs = jnp.concatenate(
            [
                jnp.concatenate(
                    [res_s[:, at : at + LANES], res_s[:, beside : beside + LANES]], axis=0
                ),
                ones,
            ],
            axis=1,
        )

        def one(u, carry, rhs=rhs, t=t):
            acc, cnt = carry
            m = t * per + u
            code = jnp.broadcast_to(codes_t[pl.ds(m, 1), :], (words, 2 * slots)).astype(bf16)
            onehot = jnp.where(code == word, jnp.ones_like(word), jnp.zeros_like(word))
            prod = dot(onehot, rhs)
            first = u * sub_width
            acc = jnp.where((lanes >= first) & (lanes < first + sub_width), prod[:, :LANES], acc)
            cnt = jnp.where(lanes == m, prod[:, LANES:], cnt)
            return acc, cnt

        acc, counts = lax.fori_loop(
            0, per, one, (jnp.zeros((words, LANES), f32), counts), unroll=4
        )
        put(t, acc)
    put(tiles, counts)

    for t in range(tiles + 1):
        pair_copy(t).wait_recv()
        sum_s[:, :, t * LANES : (t + 1) * LANES] = pair_s[t, core] + pair_r[t]
    start_own(sum_s, sum_r, 3, chip)

    def send_sum(d, carry):
        other = lax.rem(chip + d, chips)
        pltpu.make_async_remote_copy(
            src_ref=sum_s.at[other],
            dst_ref=sum_r.at[chip],
            send_sem=send_sem.at[3],
            recv_sem=recv_sem.at[3],
            device_id={"cent": other * 2 + core},
        ).start()
        return carry

    lax.fori_loop(1, chips, send_sum, 0)

    for i in range(2):
        at = slice(i * half, (i + 1) * half)
        resid_ref[:, at] = (
            dot(place_s[0], res_s[:, at], 0, 0) + dot(place_s[1 + i], res_s[:, width:], 0, 0)
        ).astype(bf16)
    arrived(rows_r, 2)
    held_counts = dot(pick_a, ones[:slots], 0, 0) + dot(pick_b, ones[:slots], 0, 0) + prior_weight
    rest = rows_r[:, :, width:].reshape(slots, half)
    main = rows_r[:, :, :width].reshape(slots, width)
    for i, pick in enumerate((pick_b, pick_c)):
        coarse = dot(pick_a, main[:, i * half : (i + 1) * half], 0, 0) + dot(pick, rest, 0, 0)
        for t in range(half // LANES):
            cut = slice(t * LANES, (t + 1) * LANES)
            at = slice(i * half + t * LANES, i * half + (t + 1) * LANES)
            newc_ref[:, at] = (
                coarse[:, cut] + prior_weight * cent_ref[:, at].astype(f32)
            ) / held_counts

    arrived(sum_r, 3)
    totals = jnp.sum(sum_r[...], axis=0)
    col = lax.broadcasted_iota(jnp.int32, (LANES, width), 1)
    row = lax.broadcasted_iota(jnp.int32, (LANES, width), 0) * sub_width
    expand = ((col >= row) & (col < row + sub_width)).astype(f32)
    spread = dot(totals[:, width:], expand, precision=lax.Precision.HIGHEST)
    newb_ref[...] = (totals[:, :width] + prior_weight * book_ref[...]) / (spread + prior_weight)
    sent(ids_s, 0)
    sent(ans_s, 1)
    sent(rows_s, 2)
    sent(sum_s, 3)
    for t in range(tiles + 1):
        pair_copy(t).wait_send()


def shards(embeddings, assign, codes, centroids, codebook):
    num_rows, width = embeddings.shape
    held = centroids.shape[0]
    mine = codebook.shape[0]
    subspaces = codes.shape[1]
    peers = lax.axis_size("cent")
    slots = peers * FULL
    long = width + width // 2
    tiles = width // LANES + 1
    vmem = pl.BlockSpec(memory_space=pltpu.VMEM)
    return pl.pallas_call(
        functools.partial(step_kernel, peers),
        out_shape=(
            jax.ShapeDtypeStruct((num_rows, width), bf16),
            jax.ShapeDtypeStruct((held, width), f32),
            jax.ShapeDtypeStruct((mine, width), f32),
        ),
        in_specs=[vmem] * 5,
        out_specs=(vmem,) * 3,
        scratch_shapes=[
            pltpu.VMEM((peers, FULL, 2 * LANES), bf16),
            pltpu.VMEM((peers, FULL, 2 * LANES), bf16),
            pltpu.VMEM((peers, FULL, long), bf16),
            pltpu.VMEM((peers, FULL, long), bf16),
            pltpu.VMEM((peers, FULL, long), bf16),
            pltpu.VMEM((peers, FULL, long), bf16),
            pltpu.VMEM((tiles, 2, peers // 2, mine, LANES), f32),
            pltpu.VMEM((tiles, peers // 2, mine, LANES), f32),
            pltpu.VMEM((peers // 2, mine, width + LANES), f32),
            pltpu.VMEM((peers // 2, mine, width + LANES), f32),
            pltpu.VMEM((3, slots, num_rows), bf16),
            pltpu.VMEM((subspaces, 2 * slots), f32),
            pltpu.VMEM((slots, long), bf16),
            pltpu.SemaphoreType.DMA((4,)),
            pltpu.SemaphoreType.DMA((4,)),
            pltpu.SemaphoreType.DMA((tiles,)),
            pltpu.SemaphoreType.DMA((tiles,)),
        ],
        compiler_params=pltpu.CompilerParams(
            collective_id=0, has_side_effects=True, vmem_limit_bytes=48 * 1024 * 1024
        ),
    )(assign.reshape(1, num_rows), embeddings, codes, centroids, codebook)


def solution(mesh):
    spec = P(("group", "cent"), None)
    in_specs = (spec, P(("group", "cent")), spec, spec, spec)
    return jax.shard_map(
        shards, mesh=mesh, in_specs=in_specs, out_specs=(spec, spec, spec), check_vma=False
    )
```

time: 73 us -> 62.6 us (0.86)
  the two profiles are of different devices: /device:TPU:13 before, /device:TPU:20 now
where the time goes in v3:
time: 62.6 us; the launch traced here: 62.3 us
  Pallas kernels  55.6 us (89%)
  local copies, waits for them, and re-layouts  6.09 us (10%)
  between operations  0.66 us (1%)
    pallas_call x1, Pallas kernels, shards(): pl.pallas_call(functools.partial(step_kernel, peers), out_shape=(jax.Shap...  55.6 us
    unnamed x10, local copies, waits for them, and re-layouts  5.4 us

profile of v3, /device:TPU:20, one launch (start us, length us, event | category | flops | bytes accessed | tf_op | source)
XLA Modules:
  0.0 62.3 jit_solution(6230140348447098080)
XLA Ops:
  0.6 0.7 %reshape.9.assign_ref = s32[1,384]{1,0:T(1,128)S(1)} reshape(s32[384]{0:T(512)} %param.6) | data formatting | bytes 3072 | tf_op jit(solution)/shard_map/reshape | solution.py:333
  1.3 0.0 copy-start.2
  1.3 1.0 %copy.8.codes_ref = s32[384,96]{1,0:T(8,128)S(1)} copy(s32[384,96]{0,1:T(8,128)} %param.7) | data formatting | bytes 294912 | tf_op args[2]
  2.4 0.0 copy-done.2
  2.4 0.0 copy-start
  2.4 1.1 %copy-done = bf16[384,768]{1,0:T(8,128)(2,1)S(1)} copy-done((bf16[384,768]{1,0:T(8,128)(2,1)S(1)}, bf16[384,768]{1,0:T(8,128)(2,1)}, u32[]{:S(2)}) %copy-start) | copy-done | bytes 589848
  3.4 0.0 copy-start.1
  3.4 1.0 %copy-done.1 = bf16[256,768]{1,0:T(8,128)(2,1)S(1)} copy-done((bf16[256,768]{1,0:T(8,128)(2,1)S(1)}, bf16[256,768]{1,0:T(8,128)(2,1)}, u32[]{:S(2)}) %copy-start.1) | copy-done | bytes 393240
  4.4 55.6 %shard_map.76 = (bf16[384,768]{1,0:T(8,128)(2,1)S(1)}, f32[256,768]{1,0:T(8,128)S(1)}, f32[8,768]{1,0:T(8,128)S(1)}) custom-call(s32[1,384]{1,0:T(1,128)S(1)} %reshape.9.assign_ref, bf16[384,768]{1,0:T(8,128)(2,1)S(1)} %copy-done, s32[384,96]{1,0:T(8,128)S(1)} %copy.8.codes_ref, bf16[256,768]{1,0:T(8,128)(2,1)S(1)} %copy-done.1, f32[8,768]{1,0:T(8,128)S(1)} %copy-done.2), custom_call_target="tpu_custom_call" | custom-call | tf_op jit(solution)/shard_map/pallas_call | solution.py:302
  60.0 0.8 %copy.12 = bf16[384,768]{1,0:T(8,128)(2,1)} copy(bf16[384,768]{1,0:T(8,128)(2,1)S(1)} %get-tuple-element.6) | data formatting | bytes 1179648
  60.8 0.9 %copy.13 = f32[256,768]{1,0:T(8,128)} copy(f32[256,768]{1,0:T(8,128)S(1)} %get-tuple-element.7) | data formatting | bytes 1572864
  61.7 0.6 copy.14
Async XLA Ops:
  1.3 1.0 %copy-start.2 = (f32[8,768]{1,0:T(8,128)S(1)}, f32[8,768]{1,0:T(8,128)}, u32[]{:S(2)}) copy-start(f32[8,768]{1,0:T(8,128)} %book_ref.1) | copy-start | bytes 73732
  2.4 1.1 %copy-start = (bf16[384,768]{1,0:T(8,128)(2,1)S(1)}, bf16[384,768]{1,0:T(8,128)(2,1)}, u32[]{:S(2)}) copy-start(bf16[384,768]{1,0:T(8,128)(2,1)} %emb_ref.1) | copy-start | bytes 1769476
  3.4 1.0 %copy-start.1 = (bf16[256,768]{1,0:T(8,128)(2,1)S(1)}, bf16[256,768]{1,0:T(8,128)(2,1)}, u32[]{:S(2)}) copy-start(bf16[256,768]{1,0:T(8,128)(2,1)} %cent_ref.1) | copy-start | bytes 1179652

commit v4 on v3

--- a/solution.py
+++ b/solution.py
@@ -10,7 +10,6 @@
 CAP = 12
 FULL = 8
 REST = CAP - FULL
-EARLY = 9
 LANES = 128
 
 prior_weight = 16.0
@@ -27,9 +26,9 @@
 def step_kernel(
     peers,
     assign_ref,
-    emb_ref,
+    emb_any,
     codes_ref,
-    cent_ref,
+    cent_any,
     book_ref,
     resid_ref,
     newc_ref,
@@ -46,7 +45,12 @@
     sum_r,
     place_s,
     codes_t,
-    res_s,
+    res_t,
+    sums_t,
+    counts_t,
+    emb_ref,
+    cent_ref,
+    load_sem,
     send_sem,
     recv_sem,
     pair_send,
@@ -55,7 +59,7 @@
     me = lax.axis_index("cent")
     num_rows, width = emb_ref.shape
     half = width // 2
-    subspaces = codes_ref.shape[1]
+    subspaces = codes_ref.shape[0]
     sub_width = width // subspaces
     held = cent_ref.shape[0]
     mine = book_ref.shape[0]
@@ -66,6 +70,11 @@
     chip = lax.div(me, 2)
     tiles = width // LANES
 
+    load_emb = pltpu.make_async_copy(emb_any, emb_ref, load_sem.at[0])
+    load_cent = pltpu.make_async_copy(cent_any, cent_ref, load_sem.at[1])
+    load_emb.start()
+    load_cent.start()
+    counts_t[...] = jnp.zeros_like(counts_t)
     barrier = pltpu.get_barrier_semaphore()
 
     def greet(d, carry):
@@ -132,6 +141,7 @@
     start_own(ids_s, ids_r, 0, me)
     start_sends(ids_s, ids_r, 0, 1, peers)
 
+    load_emb.wait()
     emb = emb_ref[...]
     rows_s[:, :, :width] = dot(places[0], emb).astype(bf16).reshape(peers, FULL, width)
     rows_s[:, :, width:] = (
@@ -140,12 +150,11 @@
         .reshape(peers, FULL, half)
     )
     start_own(rows_s, rows_r, 2, me)
-    start_sends(rows_s, rows_r, 2, 1, EARLY)
     shifted = (codes_ref[...] + 1).astype(f32).astype(bf16)
     lower = lax.broadcasted_iota(jnp.int32, (subspaces, slots), 0) < subspaces // 2
-    codes_t[:, :slots] = dot(shifted, places[0], 0, 1)
+    codes_t[:, :slots] = dot(shifted, places[0], 1, 1)
     codes_t[:, slots:] = jnp.where(
-        lower, dot(shifted, places[1], 0, 1), dot(shifted, places[2], 0, 1)
+        lower, dot(shifted, places[1], 1, 1), dot(shifted, places[2], 1, 1)
     )
 
     arrived(ids_r, 0)
@@ -166,6 +175,7 @@
     front = lax.broadcasted_iota(jnp.int32, got_b.shape, 1) < REST
     pick_b = pick_of(jnp.where(front, got_b.astype(f32), 0.0))
     pick_c = pick_of(jnp.where(front, 0.0, got_b.astype(f32)))
+    load_cent.wait()
     cent = cent_ref[...]
     ans_s[:, :, :width] = dot(pick_a, cent).astype(bf16).reshape(peers, FULL, width)
     ans_s[:, :, width:] = (
@@ -175,19 +185,20 @@
     )
     start_own(ans_s, ans_r, 1, me)
     start_sends(ans_s, ans_r, 1, 1, peers)
-    start_sends(rows_s, rows_r, 2, EARLY, peers)
+    start_sends(rows_s, rows_r, 2, 1, peers)
 
     arrived(ans_r, 1)
-    res_s[...] = (
+    res = (
         rows_s[...].reshape(slots, width + half).astype(f32)
         - ans_r[...].reshape(slots, width + half).astype(f32)
-    ).astype(bf16)
+    )
+    res_t[...] = res.T
+    res = res.astype(bf16)
 
     per = LANES // sub_width
     word = (lax.broadcasted_iota(jnp.int32, (words, 2 * slots), 0) + 1).astype(f32).astype(bf16)
-    lanes = lax.broadcasted_iota(jnp.int32, (words, LANES), 1)
     ones = jnp.ones((2 * slots, LANES), bf16)
-    counts = jnp.zeros((words, LANES), f32)
+    plain = jnp.ones((sub_width, 2 * slots), f32)
 
     def pair_copy(t):
         return pltpu.make_async_remote_copy(
@@ -209,34 +220,25 @@
         pair_copy(t).start()
 
     for t in range(tiles):
-        at = t * LANES
-        beside = width + at % half
-        rhs = jnp.concatenate(
-            [
-                jnp.concatenate(
-                    [res_s[:, at : at + LANES], res_s[:, beside : beside + LANES]], axis=0
-                ),
-                ones,
-            ],
-            axis=1,
-        )
-
-        def one(u, carry, rhs=rhs, t=t):
-            acc, cnt = carry
+
+        def one(u, carry, t=t):
             m = t * per + u
+            at = pl.multiple_of(m * sub_width, sub_width)
+            beside = pl.multiple_of(width + t * LANES % half + u * sub_width, sub_width)
+            part = jnp.concatenate(
+                [res_t[pl.ds(at, sub_width), :], res_t[pl.ds(beside, sub_width), :]], axis=1
+            )
+            lhs = jnp.concatenate([part, plain], axis=0).astype(bf16)
             code = jnp.broadcast_to(codes_t[pl.ds(m, 1), :], (words, 2 * slots)).astype(bf16)
             onehot = jnp.where(code == word, jnp.ones_like(word), jnp.zeros_like(word))
-            prod = dot(onehot, rhs)
-            first = u * sub_width
-            acc = jnp.where((lanes >= first) & (lanes < first + sub_width), prod[:, :LANES], acc)
-            cnt = jnp.where(lanes == m, prod[:, LANES:], cnt)
-            return acc, cnt
-
-        acc, counts = lax.fori_loop(
-            0, per, one, (jnp.zeros((words, LANES), f32), counts), unroll=4
-        )
-        put(t, acc)
-    put(tiles, counts)
+            prod = dot(lhs, onehot, 1, 1)
+            sums_t[pl.ds(at, sub_width), :] = prod[:sub_width]
+            counts_t[pl.ds(m, 1), :] = prod[sub_width : sub_width + 1]
+            return carry
+
+        lax.fori_loop(0, per, one, 0, unroll=16)
+        put(t, sums_t[t * LANES : (t + 1) * LANES, :].T)
+    put(tiles, counts_t[...].T)
 
     for t in range(tiles + 1):
         pair_copy(t).wait_recv()
@@ -259,7 +261,7 @@
     for i in range(2):
         at = slice(i * half, (i + 1) * half)
         resid_ref[:, at] = (
-            dot(place_s[0], res_s[:, at], 0, 0) + dot(place_s[1 + i], res_s[:, width:], 0, 0)
+            dot(place_s[0], res[:, at], 0, 0) + dot(place_s[1 + i], res[:, width:], 0, 0)
         ).astype(bf16)
     arrived(rows_r, 2)
     held_counts = dot(pick_a, ones[:slots], 0, 0) + dot(pick_b, ones[:slots], 0, 0) + prior_weight
@@ -298,6 +300,7 @@
     slots = peers * FULL
     long = width + width // 2
     tiles = width // LANES + 1
+    anywhere = pl.BlockSpec(memory_space=pl.ANY)
     vmem = pl.BlockSpec(memory_space=pltpu.VMEM)
     return pl.pallas_call(
         functools.partial(step_kernel, peers),
@@ -306,7 +309,7 @@
             jax.ShapeDtypeStruct((held, width), f32),
             jax.ShapeDtypeStruct((mine, width), f32),
         ),
-        in_specs=[vmem] * 5,
+        in_specs=[vmem, anywhere, vmem, anywhere, vmem],
         out_specs=(vmem,) * 3,
         scratch_shapes=[
             pltpu.VMEM((peers, FULL, 2 * LANES), bf16),
@@ -321,7 +324,12 @@
             pltpu.VMEM((peers // 2, mine, width + LANES), f32),
             pltpu.VMEM((3, slots, num_rows), bf16),
             pltpu.VMEM((subspaces, 2 * slots), f32),
-            pltpu.VMEM((slots, long), bf16),
+            pltpu.VMEM((long, slots), f32),
+            pltpu.VMEM((width, mine * peers), f32),
+            pltpu.VMEM((LANES, mine * peers), f32),
+            pltpu.VMEM((num_rows, width), bf16),
+            pltpu.VMEM((held, width), bf16),
+            pltpu.SemaphoreType.DMA((2,)),
             pltpu.SemaphoreType.DMA((4,)),
             pltpu.SemaphoreType.DMA((4,)),
             pltpu.SemaphoreType.DMA((tiles,)),
@@ -330,7 +338,7 @@
         compiler_params=pltpu.CompilerParams(
             collective_id=0, has_side_effects=True, vmem_limit_bytes=48 * 1024 * 1024
         ),
-    )(assign.reshape(1, num_rows), embeddings, codes, centroids, codebook)
+    )(assign.reshape(1, num_rows), embeddings, codes.T, centroids, codebook)
 
 
 def solution(mesh):

time: 62.6 us -> 57.9 us (0.925)
  Pallas kernels: 55.6 us -> 50.3 us
    pallas_call x1, Pallas kernels: 55.6 us -> 50.3 us  [shards(): pl.pallas_call(functools.partial(step_kernel, peers), out_shape=(jax.Shap...]
    unnamed x10 -> x11, local copies, waits for them, and re-layouts: 5.4 us -> 6.01 us
where the time goes in v4:
time: 57.9 us; the launch traced here: 57.6 us
  Pallas kernels  50.3 us (87%)
  local copies, waits for them, and re-layouts  6.69 us (12%)
  between operations  0.64 us (1%)
    pallas_call x1, Pallas kernels, shards(): pl.pallas_call(functools.partial(step_kernel, peers), out_shape=(jax.Shap...  50.3 us
    unnamed x11, local copies, waits for them, and re-layouts  6.01 us

profile of v4, /device:TPU:20, one launch (start us, length us, event | category | flops | bytes accessed | tf_op | source)
XLA Modules:
  0.0 57.6 jit_solution(2635640767752997858)
XLA Ops:
  0.6 0.7 %reshape.9.assign_ref = s32[1,384]{1,0:T(1,128)S(1)} reshape(s32[384]{0:T(512)} %param.6) | data formatting | bytes 3072 | tf_op jit(solution)/shard_map/reshape | solution.py:341
  1.3 0.0 copy-start
  1.3 1.1 %copy-done = bf16[384,768]{1,0:T(8,128)(2,1)S(1)} copy-done((bf16[384,768]{1,0:T(8,128)(2,1)S(1)}, bf16[384,768]{1,0:T(8,128)(2,1)}, u32[]{:S(2)}) %copy-start) | copy-done | bytes 589848
  2.4 0.0 copy-start.1
  2.4 1.0 %copy-done.1 = bf16[256,768]{1,0:T(8,128)(2,1)S(1)} copy-done((bf16[256,768]{1,0:T(8,128)(2,1)S(1)}, bf16[256,768]{1,0:T(8,128)(2,1)}, u32[]{:S(2)}) %copy-start.1) | copy-done | bytes 393240
  3.4 0.0 copy-start.2
  3.4 0.9 %copy-done.2 = s32[384,96]{0,1:T(8,128)S(1)} copy-done((s32[384,96]{0,1:T(8,128)S(1)}, s32[384,96]{0,1:T(8,128)}, u32[]{:S(2)}) %copy-start.2) | copy-done | bytes 147480
  4.3 0.0 copy-start.3
  4.3 0.7 %copy-done.3 = f32[8,768]{1,0:T(8,128)S(1)} copy-done((f32[8,768]{1,0:T(8,128)S(1)}, f32[8,768]{1,0:T(8,128)}, u32[]{:S(2)}) %copy-start.3) | copy-done | bytes 24600
  5.0 50.3 %shard_map.76 = (bf16[384,768]{1,0:T(8,128)(2,1)S(1)}, f32[256,768]{1,0:T(8,128)S(1)}, f32[8,768]{1,0:T(8,128)S(1)}) custom-call(s32[1,384]{1,0:T(1,128)S(1)} %reshape.9.assign_ref, bf16[384,768]{1,0:T(8,128)(2,1)S(1)} %copy-done, s32[96,384]{1,0:T(8,128)S(1)} %bitcast.1, bf16[256,768]{1,0:T(8,128)(2,1)S(1)} %copy-done.1, f32[8,768]{1,0:T(8,128)S(1)} %copy-done.3), custom_call_target="tpu_custom_call" | custom-call | tf_op jit(solution)/shard_map/pallas_call | solution.py:305
  55.3 0.8 %copy.11 = bf16[384,768]{1,0:T(8,128)(2,1)} copy(bf16[384,768]{1,0:T(8,128)(2,1)S(1)} %get-tuple-element.6) | data formatting | bytes 1179648
  56.1 0.9 %copy.12 = f32[256,768]{1,0:T(8,128)} copy(f32[256,768]{1,0:T(8,128)S(1)} %get-tuple-element.7) | data formatting | bytes 1572864
  57.0 0.6 %copy.13 = f32[8,768]{1,0:T(8,128)} copy(f32[8,768]{1,0:T(8,128)S(1)} %get-tuple-element.8) | data formatting | bytes 49152
Async XLA Ops:
  1.3 1.1 %copy-start = (bf16[384,768]{1,0:T(8,128)(2,1)S(1)}, bf16[384,768]{1,0:T(8,128)(2,1)}, u32[]{:S(2)}) copy-start(bf16[384,768]{1,0:T(8,128)(2,1)} %emb_any.1) | copy-start | bytes 1769476
  2.4 1.0 %copy-start.1 = (bf16[256,768]{1,0:T(8,128)(2,1)S(1)}, bf16[256,768]{1,0:T(8,128)(2,1)}, u32[]{:S(2)}) copy-start(bf16[256,768]{1,0:T(8,128)(2,1)} %cent_any.1) | copy-start | bytes 1179652
  3.4 0.9 %copy-start.2 = (s32[384,96]{0,1:T(8,128)S(1)}, s32[384,96]{0,1:T(8,128)}, u32[]{:S(2)}) copy-start(s32[384,96]{0,1:T(8,128)} %param.7) | copy-start | bytes 442372
  4.3 0.7 %copy-start.3 = (f32[8,768]{1,0:T(8,128)S(1)}, f32[8,768]{1,0:T(8,128)}, u32[]{:S(2)}) copy-start(f32[8,768]{1,0:T(8,128)} %book_ref.1) | copy-start | bytes 73732
